TPU v7x, 256 devices: a whole 4x4x8 slice. The times are simulated.
256 devices in a mesh: replica: 2 (over z_lo), segment: 4 (over z_hi), tensor: 32 (over x, y, core).
Axes of the slice: x: 4, y: 4, z: 8 (z_hi: 4, z_lo: 2; z = z_hi * 2 + z_lo), core: 2. Of those that a mesh axis runs over, the one named last changes fastest.
Arguments:
- x_in: bfloat16 [256, 8192], P('replica', 'tensor'), parts along dimension 0, may hold values from -6 to 6
- norm_gain: float32 [4, 8192], P('segment'), may hold values from 0.5 to 1.5
- in_index: int32 [4, 224, 72], P('segment', 'tensor'), may hold values from -1 to 127, as said below
- gate_blocks: bfloat16 [4, 224, 72, 4096], P('segment', 'tensor'), may hold values from -0.09375 to 0.09375
- up_blocks: bfloat16 [4, 224, 72, 4096], P('segment', 'tensor'), may hold values from -0.09375 to 0.09375
- out_index: int32 [4, 128, 126], P('segment', 'tensor'), may hold values from -1 to 223, as said below
- down_blocks: bfloat16 [4, 128, 126, 4096], P('segment', 'tensor'), may hold values from -0.0625 to 0.0625
Outputs:
- sections: bfloat16 [4, 256, 8192], P('segment', 'replica', 'tensor'), parts along dimension 1
There are 2 independent parts, one for each index of `replica`. A program takes and returns all parts, laid end to end along the dimension named above; an argument that names none is the same for every part. Nothing has to cross between parts.
Inputs may be any that keep to these rules, and one draw needn't show every extreme that they name: `in_index`: for each section and column block the entries name distinct row blocks, the kept ones first and -1 in the remaining slots; between 3 * 128 / 8 (rounded down) and 72 slots are kept, and in every section some column block keeps exactly 72 and another exactly the least. `out_index`: for each section and column block the entries name distinct row blocks, the kept ones first and -1 in the remaining slots; between 3 * 224 / 8 (rounded down) and 126 slots are kept, and in every section some column block keeps exactly 126 and another exactly the least.
All inputs are finite; a program needn't handle non-finite values.
Results may differ from a plain program's by a relative error of at most 0.0095.
Values may be sent and summed in bfloat16 or wider, within the bound.
No kernel may reach another device: no remote copies, remote signals or barrier semaphores. Data moves between devices by JAX's collectives and lax.ppermute only.
A program may use at most 128 MiB of HBM per device.

v0:
```python
import jax
import jax.numpy as jnp
from jax import lax
from jax.sharding import PartitionSpec as P

D = 8192
FFW = 14336
BS = 64


def shifted(value, axis, by):
    length = lax.axis_size(axis)
    pairs = [(i, i + by) for i in range(length) if 0 <= i + by < length]
    return lax.ppermute(value, axis, pairs)


def densify(index, blocks, row_blocks):
    tile_count = index.shape[0]
    picks = (index[:, None, :] == jnp.arange(row_blocks, dtype=jnp.int32)[None, :, None]).astype(
        jnp.bfloat16
    )
    dense = jnp.einsum("crm,cmq->crq", picks, blocks, preferred_element_type=jnp.bfloat16)
    dense = dense.reshape(tile_count, row_blocks, BS, BS)
    return jnp.transpose(dense, (1, 2, 0, 3)).reshape(row_blocks * BS, tile_count * BS)


def local(x_in, norm_gain, in_index, gate_blocks, up_blocks, out_index, down_blocks):
    segment_count = lax.axis_size("segment")
    segment_at = lax.axis_index("segment")
    tokens, local_cols = x_in.shape
    gain_row = norm_gain[0]
    index_in = in_index[0]
    index_out = out_index[0]
    gate_dense = densify(index_in, gate_blocks[0], D // BS)
    up_dense = densify(index_in, up_blocks[0], D // BS)
    down_dense = densify(index_out, down_blocks[0], FFW // BS)
    rows_micro = tokens // 2
    group_count = tokens // rows_micro
    tick_count = group_count + segment_count - 1
    result = jnp.zeros((tokens, local_cols), jnp.bfloat16)
    carried = jnp.zeros((rows_micro, local_cols), jnp.bfloat16)
    for tick_now in range(tick_count):
        first_group = min(tick_now, group_count - 1)
        first_rows = x_in[first_group * rows_micro : (first_group + 1) * rows_micro]
        incoming = jnp.where(segment_at == 0, first_rows, carried)
        whole = lax.all_gather(incoming, "tensor", axis=1, tiled=True)
        wide = whole.astype(jnp.float32)
        stat = jnp.mean(wide * wide, axis=1, keepdims=True)
        section_normed = (wide * lax.rsqrt(stat + 1e-05) * gain_row[None, :]).astype(jnp.bfloat16)
        gate = jnp.dot(section_normed, gate_dense, preferred_element_type=jnp.float32)
        up_part = jnp.dot(section_normed, up_dense, preferred_element_type=jnp.float32)
        section_hidden = (jax.nn.silu(gate) * up_part).astype(jnp.bfloat16)
        mixed = jnp.dot(
            lax.all_gather(section_hidden, "tensor", axis=1, tiled=True),
            down_dense,
            preferred_element_type=jnp.float32,
        )
        produced = (incoming.astype(jnp.float32) + mixed).astype(jnp.bfloat16)
        micro_id = tick_now - segment_at
        is_valid = jnp.logical_and(micro_id >= 0, micro_id < group_count)
        offset = jnp.clip(micro_id, 0, group_count - 1) * rows_micro
        previous = lax.dynamic_slice_in_dim(result, offset, rows_micro, 0)
        result = lax.dynamic_update_slice_in_dim(
            result, jnp.where(is_valid, produced, previous), offset, 0
        )
        if tick_now + 1 < tick_count:
            carried = shifted(produced, "segment", 1)
    return result[None]


def solution(mesh):
    placed = (
        P("replica", "tensor"),
        P("segment", None),
        P("segment", "tensor", None),
        P("segment", "tensor", None, None),
        P("segment", "tensor", None, None),
        P("segment", "tensor", None),
        P("segment", "tensor", None, None),
    )
    return jax.shard_map(
        local,
        mesh=mesh,
        in_specs=placed,
        out_specs=P("segment", "replica", "tensor"),
        check_vma=False,
    )
```

profile of v0, /device:TPU:1, one launch (start us, length us, event | category | flops | bytes accessed | tf_op | source)
XLA Modules:
  0.0 696.2 jit_solution(13553117329584117888)
XLA Ops:
  8.7 7.7 %fusion.4 = bf16[7,128,4096]{1,2,0:T(8,128)(2,1)} fusion(bf16[1,7,72,4096]{3,2,1,0:T(8,128)(2,1)} %param.10, s32[7,72]{1,0:T(8,128)S(1)} %bitcast.103), kind=kOutput, calls=%fused_computation.4 | convolution fusion | flops 528546816 | bytes 11470816 | tf_op jit(solution)/shard_map/crm,cmq->crq/dot_general | solution.py:22
  16.4 15.6 %copy.22 = bf16[128,64,7,64]{1,0,3,2:T(8,128)(2,1)} copy(bf16[128,64,7,64]{0,3,1,2:T(8,128)(2,1)} %bitcast.90) | data formatting | bytes 14680064 | tf_op jit(solution)/shard_map/transpose | solution.py:24
  32.0 20.0 %reshape.63 = bf16[8192,448]{0,1:T(8,128)(2,1)} reshape(bf16[128,64,7,64]{1,0,3,2:T(8,128)(2,1)} %copy.22) | data formatting | bytes 14680064 | tf_op jit(solution)/shard_map/reshape | solution.py:24
  52.0 7.7 %fusion.2 = bf16[7,128,4096]{1,2,0:T(8,128)(2,1)} fusion(bf16[1,7,72,4096]{3,2,1,0:T(8,128)(2,1)} %param.11, s32[7,72]{1,0:T(8,128)S(1)} %bitcast.104), kind=kOutput, calls=%fused_computation.2 | convolution fusion | flops 528546816 | bytes 11470816 | tf_op jit(solution)/shard_map/crm,cmq->crq/dot_general | solution.py:22
  59.7 15.6 %copy.24 = bf16[128,64,7,64]{1,0,3,2:T(8,128)(2,1)} copy(bf16[128,64,7,64]{0,3,1,2:T(8,128)(2,1)} %bitcast.89) | data formatting | bytes 14680064 | tf_op jit(solution)/shard_map/transpose | solution.py:24
  75.3 20.0 %reshape.65 = bf16[8192,448]{0,1:T(8,128)(2,1)} reshape(bf16[128,64,7,64]{1,0,3,2:T(8,128)(2,1)} %copy.24) | data formatting | bytes 14680064 | tf_op jit(solution)/shard_map/reshape | solution.py:24
  105.9 9.4 %fusion = bf16[4,224,4096]{1,2,0:T(8,128)(2,1)} fusion(bf16[4,126,4096]{2,0,1:T(4,128)(2,1)} %bitcast.91, s32[4,126]{1,0:T(4,128)S(1)} %bitcast.105), kind=kOutput, calls=%fused_computation | convolution fusion | flops 924956928 | bytes 11470816 | tf_op jit(solution)/shard_map/crm,cmq->crq/dot_general | solution.py:22
  115.3 17.4 %copy.28 = bf16[224,64,4,64]{1,0,3,2:T(8,128)(2,1)} copy(bf16[224,64,4,64]{0,3,1,2:T(8,128)(2,1)} %bitcast.88) | data formatting | bytes 14680064 | tf_op jit(solution)/shard_map/transpose | solution.py:24
  132.7 18.5 %reshape.67 = bf16[14336,256]{0,1:T(8,128)(2,1)} reshape(bf16[224,64,4,64]{1,0,3,2:T(8,128)(2,1)} %copy.28) | data formatting | bytes 14680064 | tf_op jit(solution)/shard_map/reshape | solution.py:24
  151.2 7.3 %all-gather.26.cloned.1.call-done = bf16[32,448,64]{1,2,0:T(8,128)(2,1)} async-done(((bf16[1,448,64]{1,2,0:T(8,128)(2,1)}), bf16[32,448,64]{1,2,0:T(8,128)(2,1)}) %all-gather.26.cloned.1.call-update) | async-done | bytes 1835024 | tf_op jit(solution)/shard_map/all_gather | solution.py:54
  164.7 6.0 select_dynamic-update-slice_fusion.3
  176.8 49.8 %all-gather.18.cloned.1.call-done = bf16[64,8192]{1,0:T(8,128)(2,1)} async-done(((bf16[64,256]{1,0:T(8,128)(2,1)}), bf16[64,8192]{1,0:T(8,128)(2,1)}) %all-gather.18.cloned.1.call-update) | async-done | bytes 1048592 | tf_op jit(solution)/shard_map/all_gather | solution.py:46
  233.9 6.0 fusion.46
  240.0 48.1 %all-gather.28.cloned.1.call-done = bf16[32,448,64]{1,2,0:T(8,128)(2,1)} async-done(((bf16[1,448,64]{1,2,0:T(8,128)(2,1)}), bf16[32,448,64]{1,2,0:T(8,128)(2,1)}) %all-gather.28.cloned.1.call-update) | async-done | bytes 1835024 | tf_op jit(solution)/shard_map/all_gather | solution.py:54
  294.2 6.0 select_dynamic-update-slice_fusion.2
  306.0 50.0 %all-gather.20.cloned.1.call-done = bf16[64,8192]{1,0:T(8,128)(2,1)} async-done(((bf16[64,256]{1,0:T(8,128)(2,1)}), bf16[64,8192]{1,0:T(8,128)(2,1)}) %all-gather.20.cloned.1.call-update) | async-done | bytes 1048592 | tf_op jit(solution)/shard_map/all_gather | solution.py:46
  369.8 47.7 %all-gather.30.cloned.1.call-done = bf16[32,448,64]{1,2,0:T(8,128)(2,1)} async-done(((bf16[1,448,64]{1,2,0:T(8,128)(2,1)}), bf16[32,448,64]{1,2,0:T(8,128)(2,1)}) %all-gather.30.cloned.1.call-update) | async-done | bytes 1835024 | tf_op jit(solution)/shard_map/all_gather | solution.py:54
  423.7 6.0 select_dynamic-update-slice_fusion.1
  435.5 50.0 %all-gather.22.cloned.1.call-done = bf16[64,8192]{1,0:T(8,128)(2,1)} async-done(((bf16[64,256]{1,0:T(8,128)(2,1)}), bf16[64,8192]{1,0:T(8,128)(2,1)}) %all-gather.22.cloned.1.call-update) | async-done | bytes 1048592 | tf_op jit(solution)/shard_map/all_gather | solution.py:46
  498.9 48.1 %all-gather.32.cloned.1.call-done = bf16[32,448,64]{1,2,0:T(8,128)(2,1)} async-done(((bf16[1,448,64]{1,2,0:T(8,128)(2,1)}), bf16[32,448,64]{1,2,0:T(8,128)(2,1)}) %all-gather.32.cloned.1.call-update) | async-done | bytes 1835024 | tf_op jit(solution)/shard_map/all_gather | solution.py:54
  553.1 6.0 select_dynamic-update-slice_fusion
  565.2 49.9 %all-gather.24.cloned.1.call-done = bf16[64,8192]{1,0:T(8,128)(2,1)} async-done(((bf16[64,256]{1,0:T(8,128)(2,1)}), bf16[64,8192]{1,0:T(8,128)(2,1)}) %all-gather.24.cloned.1.call-update) | async-done | bytes 1048592 | tf_op jit(solution)/shard_map/all_gather | solution.py:46
  629.0 47.5 %all-gather.34.cloned.1.call-done = bf16[32,448,64]{1,2,0:T(8,128)(2,1)} async-done(((bf16[1,448,64]{1,2,0:T(8,128)(2,1)}), bf16[32,448,64]{1,2,0:T(8,128)(2,1)}) %all-gather.34.cloned.1.call-update) | async-done | bytes 1835024 | tf_op jit(solution)/shard_map/all_gather | solution.py:54
  682.6 6.6 fusion.52
  (94 shorter events, 115.0 us)
Async XLA Ops:
  6.5 88.8 %all-gather.16.cloned.1.call-start = ((), (), s32[]{:S(2)}) async-start(), calls=%async_computation | async-start | bytes 1081344 | tf_op jit(solution)/shard_map/all_gather | solution.py:46
  7.9 150.6 %all-gather.26.cloned.1.call-start = ((), (), s32[]{:S(2)}) async-start(), calls=%async_computation.5 | async-start | bytes 2162688 | tf_op jit(solution)/shard_map/all_gather | solution.py:54
  75.3 21.6 %copy-start.6 = (f32[1,8192]{1,0:T(1,128)S(1)}, f32[1,8192]{1,0:T(1,128)}, u32[]{:S(2)}) copy-start(f32[1,8192]{1,0:T(1,128)} %param.8) | copy-start | bytes 98308
  96.9 5.8 copy-start
  96.9 5.8 copy-start.1
  105.7 121.0 %all-gather.18.cloned.1.call-start = ((), (), s32[]{:S(2)}) async-start(), calls=%async_computation.1 | async-start | bytes 1081344 | tf_op jit(solution)/shard_map/all_gather | solution.py:46
  161.3 3.4 copy-start.12
  164.7 11.2 %copy-start.7 = (bf16[128,256]{1,0:T(8,128)(2,1)S(1)}, bf16[128,256]{1,0:T(8,128)(2,1)}, u32[]{:S(2)}) copy-start(bf16[128,256]{1,0:T(8,128)(2,1)} %param.7) | copy-start | bytes 196612
  170.7 5.2 collective-permute-start
  176.5 111.6 %all-gather.28.cloned.1.call-start = ((), (), s32[]{:S(2)}) async-start(), calls=%async_computation.6 | async-start | bytes 2162688 | tf_op jit(solution)/shard_map/all_gather | solution.py:54
  228.2 5.7 copy-start.3
  239.9 116.2 %all-gather.20.cloned.1.call-start = ((), (), s32[]{:S(2)}) async-start(), calls=%async_computation.2 | async-start | bytes 1081344 | tf_op jit(solution)/shard_map/all_gather | solution.py:46
  290.8 3.4 copy-start.10
  300.2 5.2 collective-permute-start.1
  306.0 111.6 %all-gather.30.cloned.1.call-start = ((), (), s32[]{:S(2)}) async-start(), calls=%async_computation.7 | async-start | bytes 2162688 | tf_op jit(solution)/shard_map/all_gather | solution.py:54
  357.6 5.7 copy-start.4
  369.4 116.2 %all-gather.22.cloned.1.call-start = ((), (), s32[]{:S(2)}) async-start(), calls=%async_computation.3 | async-start | bytes 1081344 | tf_op jit(solution)/shard_map/all_gather | solution.py:46
  429.7 5.2 collective-permute-start.2
  435.5 111.6 %all-gather.32.cloned.1.call-start = ((), (), s32[]{:S(2)}) async-start(), calls=%async_computation.8 | async-start | bytes 2162688 | tf_op jit(solution)/shard_map/all_gather | solution.py:54
  487.1 5.7 copy-start.5
  498.8 116.2 %all-gather.24.cloned.1.call-start = ((), (), s32[]{:S(2)}) async-start(), calls=%async_computation.4 | async-start | bytes 1081344 | tf_op jit(solution)/shard_map/all_gather | solution.py:46
  559.1 5.2 collective-permute-start.3
  565.0 111.6 %all-gather.34.cloned.1.call-start = ((), (), s32[]{:S(2)}) async-start(), calls=%async_computation.9 | async-start | bytes 2162688 | tf_op jit(solution)/shard_map/all_gather | solution.py:54
  616.6 5.7 copy-start.2
  (4 other events, 13.2 us)
Sparse Core Ops, SparseCore 0:
  9.8 51.9 all-gather.15
  105.8 52.7 all-gather.25
  176.6 49.9 all-gather.17
  240.0 48.0 all-gather.27
  306.1 49.9 all-gather.19
  369.5 48.0 all-gather.29
  435.6 49.9 all-gather.21
  499.0 48.0 all-gather.31
  565.1 49.9 all-gather.23
  628.4 48.0 all-gather.33
where the time goes:
time: 708 us; the launch traced here: 696 us
  waiting for transfers between devices  403 us (57%)
  local copies, waits for them, and re-layouts  139 us (20%)
  matrix products  111 us (16%)
  starting transfers between devices  18 us (3%)
  between operations  14 us (2%)
  other arithmetic  11.5 us (2%)
    all_gather x5, waiting for transfers between devices, local(): whole = lax.all_gather(incoming, 'tensor', axis=1, tiled=True)  200 us
    all_gather x5, waiting for transfers between devices, local(): lax.all_gather(section_hidden, 'tensor', axis=1, tiled=True)  199 us
    reshape x3, local copies, waits for them, and re-layouts, densify(): jnp.transpose(dense, (1, 2, 0, 3)).reshape(row_blocks * BS, tile_count * BS)  58.6 us
    transpose x3, local copies, waits for them, and re-layouts, densify(): jnp.transpose(dense, (1, 2, 0, 3)).reshape(row_blocks * BS, tile_count * BS)  48.6 us
    dot_general x5, matrix products, local(): jnp.dot(lax.all_gather(section_hidden, 'tensor', axis=1, tiled=True), dow...  30.6 us
    dot_general x5, matrix products, local(): jnp.dot(section_normed, gate_dense, preferred_element_type=jnp.float32)  28.7 us
    dot_general x5, matrix products, local(): jnp.dot(section_normed, up_dense, preferred_element_type=jnp.float32)  26.7 us
    dot_general x3, matrix products, densify(): jnp.einsum('crm,cmq->crq', picks, blocks, preferred_element_type=jnp.bflo...  24.9 us
  transfers between devices with their start and end apart: 14, of which 13 were waited for; matrix products, arithmetic and copies ran while one was open for 19% of the time, Pallas kernels for 0%

commit v1 on v0

--- a/solution.py
+++ b/solution.py
@@ -43,7 +43,10 @@
         first_group = min(tick_now, group_count - 1)
         first_rows = x_in[first_group * rows_micro : (first_group + 1) * rows_micro]
         incoming = jnp.where(segment_at == 0, first_rows, carried)
-        whole = lax.all_gather(incoming, "tensor", axis=1, tiled=True)
+        size = lax.axis_size("tensor")
+        pieces = jnp.stack([incoming for _ in range(size)])
+        pieces = lax.all_to_all(pieces, "tensor", split_axis=0, concat_axis=0)
+        whole = jnp.concatenate(pieces, axis=1)
         wide = whole.astype(jnp.float32)
         stat = jnp.mean(wide * wide, axis=1, keepdims=True)
         section_normed = (wide * lax.rsqrt(stat + 1e-05) * gain_row[None, :]).astype(jnp.bfloat16)

time: 708 us -> 587 us (0.83)
  waiting for transfers between devices: 403 us -> 204 us
  blocking collectives: 0 us -> 93.4 us
  matrix products: 111 us -> 84.9 us
  local copies, waits for them, and re-layouts: 139 us -> 153 us
  starting transfers between devices: 18 us -> 25.7 us
    all_gather x5 -> x0, waiting for transfers between devices: 200 us -> none  [local(): whole = lax.all_gather(incoming, 'tensor', axis=1, tiled=True)]
    all_to_all x0 -> x4, blocking collectives: none -> 93.4 us  [local(): pieces = lax.all_to_all(pieces, 'tensor', split_axis=0, concat_axis=0)]
    dot_general x5, matrix products: 28.7 us -> 14.6 us  [local(): jnp.dot(section_normed, gate_dense, preferred_element_type=jnp.float32)]
    dot_general x5, matrix products: 26.7 us -> 14.3 us  [local(): jnp.dot(section_normed, up_dense, preferred_element_type=jnp.float32)]
    all_to_all x0 -> x1, starting transfers between devices: none -> 8.58 us  [local(): pieces = lax.all_to_all(pieces, 'tensor', split_axis=0, concat_axis=0)]
    unnamed x35 -> x48, local copies, waits for them, and re-layouts: 18.1 us -> 24.5 us
  transfers between devices with their start and end apart: 14 -> 10, of which waited for: 13 -> 9; matrix products, arithmetic and copies ran while one was open for 19% -> 23% of each run, Pallas kernels for 0% -> 0%
where the time goes in v1:
time: 587 us; the launch traced here: 580 us
  waiting for transfers between devices  204 us (35%)
  local copies, waits for them, and re-layouts  153 us (26%)
  blocking collectives  93.4 us (16%)
  matrix products  84.9 us (14%)
  starting transfers between devices  25.7 us (4%)
  between operations  14 us (2%)
    all_gather x5, waiting for transfers between devices, local(): lax.all_gather(section_hidden, 'tensor', axis=1, tiled=True)  200 us
    all_to_all x4, blocking collectives, local(): pieces = lax.all_to_all(pieces, 'tensor', split_axis=0, concat_axis=0)  93.4 us
    reshape x3, local copies, waits for them, and re-layouts, densify(): jnp.transpose(dense, (1, 2, 0, 3)).reshape(row_blocks * BS, tile_count * BS)  58.6 us
    transpose x3, local copies, waits for them, and re-layouts, densify(): jnp.transpose(dense, (1, 2, 0, 3)).reshape(row_blocks * BS, tile_count * BS)  48.6 us
    dot_general x5, matrix products, local(): jnp.dot(lax.all_gather(section_hidden, 'tensor', axis=1, tiled=True), dow...  31.1 us
    dot_general x3, matrix products, densify(): jnp.einsum('crm,cmq->crq', picks, blocks, preferred_element_type=jnp.bflo...  24.9 us
    unnamed x48, local copies, waits for them, and re-layouts  24.5 us
    all_gather x5, local copies, waits for them, and re-layouts, local(): lax.all_gather(section_hidden, 'tensor', axis=1, tiled=True)  19.2 us
  transfers between devices with their start and end apart: 10, of which 9 were waited for; matrix products, arithmetic and copies ran while one was open for 23% of the time, Pallas kernels for 0%

profile of v1, /device:TPU:1, one launch (start us, length us, event | category | flops | bytes accessed | tf_op | source)
XLA Modules:
  0.0 580.4 jit_solution(6819437583407962879)
XLA Ops:
  8.4 8.6 %all-to-all-start = ((bf16[32,64,256]{2,1,0:T(8,128)(2,1)}), bf16[32,64,256]{2,1,0:T(8,128)(2,1)S(1)}, u32[]{:S(2)}, u32[]{:S(2)}) async-start(bf16[32,64,256]{2,1,0:T(8,128)(2,1)} %stack.10), calls=%async_computation | async-start | bytes 2097152 | tf_op jit(solution)/shard_map/all_to_all | solution.py:48
  19.7 7.7 %fusion.4 = bf16[7,128,4096]{1,2,0:T(8,128)(2,1)} fusion(bf16[1,7,72,4096]{3,2,1,0:T(8,128)(2,1)} %param.10, s32[7,72]{1,0:T(8,128)S(1)} %bitcast.150), kind=kOutput, calls=%fused_computation.4 | convolution fusion | flops 528546816 | bytes 11470816 | tf_op jit(solution)/shard_map/crm,cmq->crq/dot_general | solution.py:22
  27.4 15.7 %copy.23 = bf16[128,64,7,64]{1,0,3,2:T(8,128)(2,1)} copy(bf16[128,64,7,64]{0,3,1,2:T(8,128)(2,1)} %bitcast.137) | data formatting | bytes 14680064 | tf_op jit(solution)/shard_map/transpose | solution.py:24
  43.2 20.0 %reshape.193 = bf16[8192,448]{0,1:T(8,128)(2,1)} reshape(bf16[128,64,7,64]{1,0,3,2:T(8,128)(2,1)} %copy.23) | data formatting | bytes 14680064 | tf_op jit(solution)/shard_map/reshape | solution.py:24
  63.2 7.7 %fusion.2 = bf16[7,128,4096]{1,2,0:T(8,128)(2,1)} fusion(bf16[1,7,72,4096]{3,2,1,0:T(8,128)(2,1)} %param.11, s32[7,72]{1,0:T(8,128)S(1)} %bitcast.151), kind=kOutput, calls=%fused_computation.2 | convolution fusion | flops 528546816 | bytes 11470816 | tf_op jit(solution)/shard_map/crm,cmq->crq/dot_general | solution.py:22
  70.9 15.6 %copy.25 = bf16[128,64,7,64]{1,0,3,2:T(8,128)(2,1)} copy(bf16[128,64,7,64]{0,3,1,2:T(8,128)(2,1)} %bitcast.136) | data formatting | bytes 14680064 | tf_op jit(solution)/shard_map/transpose | solution.py:24
  86.5 20.0 %reshape.195 = bf16[8192,448]{0,1:T(8,128)(2,1)} reshape(bf16[128,64,7,64]{1,0,3,2:T(8,128)(2,1)} %copy.25) | data formatting | bytes 14680064 | tf_op jit(solution)/shard_map/reshape | solution.py:24
  116.1 9.5 %fusion = bf16[4,224,4096]{1,2,0:T(8,128)(2,1)} fusion(bf16[4,126,4096]{2,0,1:T(4,128)(2,1)} %bitcast.138, s32[4,126]{1,0:T(4,128)S(1)} %bitcast.152), kind=kOutput, calls=%fused_computation | convolution fusion | flops 924956928 | bytes 11470816 | tf_op jit(solution)/shard_map/crm,cmq->crq/dot_general | solution.py:22
  125.6 17.3 %copy.29 = bf16[224,64,4,64]{1,0,3,2:T(8,128)(2,1)} copy(bf16[224,64,4,64]{0,3,1,2:T(8,128)(2,1)} %bitcast.135) | data formatting | bytes 14680064 | tf_op jit(solution)/shard_map/transpose | solution.py:24
  142.9 18.5 %reshape.197 = bf16[14336,256]{0,1:T(8,128)(2,1)} reshape(bf16[224,64,4,64]{1,0,3,2:T(8,128)(2,1)} %copy.29) | data formatting | bytes 14680064 | tf_op jit(solution)/shard_map/reshape | solution.py:24
  161.4 6.1 %all-gather.11.cloned.1.call-done = bf16[32,448,64]{1,2,0:T(8,128)(2,1)} async-done(((bf16[1,448,64]{1,2,0:T(8,128)(2,1)}), bf16[32,448,64]{1,2,0:T(8,128)(2,1)}) %all-gather.11.cloned.1.call-update) | async-done | bytes 1835024 | tf_op jit(solution)/shard_map/all_gather | solution.py:57
  176.5 6.1 %select_dynamic-update-slice_fusion.3 = (bf16[128,256]{1,0:T(8,128)(2,1)S(1)}, bf16[64,256]{1,0:T(8,128)(2,1)S(1)}) fusion(bf16[128,256]{1,0:T(8,128)(2,1)S(1)} %broadcast_in_dim.6, s32[]{:T(128)S(6)} %select_n.77, pred[]{:T(512)S(6)} %and.16, bf16[14336,64]{0,1:T(8,128)(2,1)} %reshape.199, bf16[14336,256]{0,1:T(8,128)(2,1)} %reshape.197, ...), kind=kOutput, calls=%fused_computation.68 | convolution fusion | flops 469827584 | bytes 9273349 | tf_op jit(solution)/shard_map/dot_general | solution.py:56
  188.0 23.5 %all_to_all.25 = bf16[32,64,256]{2,1,0:T(8,128)(2,1)S(1)} all-to-all(bf16[32,64,256]{2,1,0:T(8,128)(2,1)S(1)} %stack.11), channel_id=1, replica_groups=mesh['replica'=2,'segment'=4,'tensor'=32] {'tensor'}, dimensions={0} | all-to-all | bytes 2097152 | tf_op jit(solution)/shard_map/all_to_all | solution.py:48
  217.5 48.6 %all-gather.13.cloned.1.call-done = bf16[32,448,64]{1,2,0:T(8,128)(2,1)} async-done(((bf16[1,448,64]{1,2,0:T(8,128)(2,1)}), bf16[32,448,64]{1,2,0:T(8,128)(2,1)}) %all-gather.13.cloned.1.call-update) | async-done | bytes 1835024 | tf_op jit(solution)/shard_map/all_gather | solution.py:57
  275.0 6.1 %select_dynamic-update-slice_fusion.2 = (bf16[128,256]{1,0:T(8,128)(2,1)S(1)}, bf16[64,256]{1,0:T(8,128)(2,1)S(1)}) fusion(bf16[128,256]{1,0:T(8,128)(2,1)S(1)} %get-tuple-element.11, s32[]{:T(128)S(6)} %select_n.80, pred[]{:T(512)S(6)} %and.17, bf16[64,256]{1,0:T(8,128)(2,1)S(1)} %broadcast_select_fusion.3, bf16[14336,64]{0,1:T(8,128)(2,1)} %reshape.201, ...), kind=kOutput, calls=%fused_computation.67 | convolution fusion | flops 469827584 | bytes 9306117 | tf_op jit(solution)/shard_map/dot_general | solution.py:56
  286.5 23.2 %all_to_all.26 = bf16[32,64,256]{2,1,0:T(8,128)(2,1)S(1)} all-to-all(bf16[32,64,256]{2,1,0:T(8,128)(2,1)S(1)} %stack.12), channel_id=1, replica_groups=mesh['replica'=2,'segment'=4,'tensor'=32] {'tensor'}, dimensions={0} | all-to-all | bytes 2097152 | tf_op jit(solution)/shard_map/all_to_all | solution.py:48
  315.7 48.6 %all-gather.15.cloned.1.call-done = bf16[32,448,64]{1,2,0:T(8,128)(2,1)} async-done(((bf16[1,448,64]{1,2,0:T(8,128)(2,1)}), bf16[32,448,64]{1,2,0:T(8,128)(2,1)}) %all-gather.15.cloned.1.call-update) | async-done | bytes 1835024 | tf_op jit(solution)/shard_map/all_gather | solution.py:57
  373.3 6.1 %select_dynamic-update-slice_fusion.1 = (bf16[128,256]{1,0:T(8,128)(2,1)S(1)}, bf16[64,256]{1,0:T(8,128)(2,1)S(1)}) fusion(bf16[128,256]{1,0:T(8,128)(2,1)S(1)} %get-tuple-element.9, s32[]{:T(128)S(6)} %select_n.84, pred[]{:T(512)S(6)} %and.18, bf16[64,256]{1,0:T(8,128)(2,1)S(1)} %broadcast_select_fusion.2, bf16[14336,64]{0,1:T(8,128)(2,1)} %reshape.203, ...), kind=kOutput, calls=%fused_computation.66 | convolution fusion | flops 469827584 | bytes 9306117 | tf_op jit(solution)/shard_map/dot_general | solution.py:56
  384.7 23.3 %all_to_all.27 = bf16[32,64,256]{2,1,0:T(8,128)(2,1)S(1)} all-to-all(bf16[32,64,256]{2,1,0:T(8,128)(2,1)S(1)} %stack.13), channel_id=1, replica_groups=mesh['replica'=2,'segment'=4,'tensor'=32] {'tensor'}, dimensions={0} | all-to-all | bytes 2097152 | tf_op jit(solution)/shard_map/all_to_all | solution.py:48
  414.0 48.6 %all-gather.17.cloned.1.call-done = bf16[32,448,64]{1,2,0:T(8,128)(2,1)} async-done(((bf16[1,448,64]{1,2,0:T(8,128)(2,1)}), bf16[32,448,64]{1,2,0:T(8,128)(2,1)}) %all-gather.17.cloned.1.call-update) | async-done | bytes 1835024 | tf_op jit(solution)/shard_map/all_gather | solution.py:57
  471.5 6.1 %select_dynamic-update-slice_fusion = (bf16[128,256]{1,0:T(8,128)(2,1)S(1)}, bf16[64,256]{1,0:T(8,128)(2,1)S(1)}) fusion(bf16[128,256]{1,0:T(8,128)(2,1)S(1)} %get-tuple-element.7, s32[]{:T(128)S(6)} %select_n.88, pred[]{:T(512)S(6)} %and.19, bf16[64,256]{1,0:T(8,128)(2,1)S(1)} %broadcast_select_fusion.1, bf16[14336,64]{0,1:T(8,128)(2,1)} %reshape.205, ...), kind=kOutput, calls=%fused_computation.65 | convolution fusion | flops 469827584 | bytes 9306117 | tf_op jit(solution)/shard_map/dot_general | solution.py:56
  483.0 23.3 %all_to_all.28 = bf16[32,64,256]{2,1,0:T(8,128)(2,1)S(1)} all-to-all(bf16[32,64,256]{2,1,0:T(8,128)(2,1)S(1)} %stack.14), channel_id=1, replica_groups=mesh['replica'=2,'segment'=4,'tensor'=32] {'tensor'}, dimensions={0} | all-to-all | bytes 2097152 | tf_op jit(solution)/shard_map/all_to_all | solution.py:48
  512.9 48.0 %all-gather.19.cloned.1.call-done = bf16[32,448,64]{1,2,0:T(8,128)(2,1)} async-done(((bf16[1,448,64]{1,2,0:T(8,128)(2,1)}), bf16[32,448,64]{1,2,0:T(8,128)(2,1)}) %all-gather.19.cloned.1.call-update) | async-done | bytes 1835024 | tf_op jit(solution)/shard_map/all_gather | solution.py:57
  567.0 6.6 %fusion.42 = bf16[1,128,256]{2,1,0:T(8,128)(2,1)} fusion(bf16[1,128,256]{2,1,0:T(8,128)(2,1)} %copy.55, s32[]{:T(128)S(6)} %select_n.92, bf16[64,256]{1,0:T(8,128)(2,1)S(1)} %broadcast_select_fusion, bf16[128,256]{1,0:T(8,128)(2,1)S(1)} %get-tuple-element.5, pred[]{:T(512)S(6)} %and.20, bf16[14336,64]{0,1:T(8,128)(2,1)} %reshape.207, ...), kind=kOutput, calls=%fused_computation.64 | convolution fusion | flops 469827584 | bytes 9273349 | tf_op jit(solution)/shard_map/dot_general | solution.py:56
  (124 shorter events, 101.3 us)
Async XLA Ops:
  8.4 98.1 %all-to-all-start = ((bf16[32,64,256]{2,1,0:T(8,128)(2,1)}), bf16[32,64,256]{2,1,0:T(8,128)(2,1)S(1)}, u32[]{:S(2)}, u32[]{:S(2)}) async-start(bf16[32,64,256]{2,1,0:T(8,128)(2,1)} %stack.10), calls=%async_computation | async-start | bytes 2097152 | tf_op jit(solution)/shard_map/all_to_all | solution.py:48
  17.0 150.6 %all-gather.11.cloned.1.call-start = ((), (), s32[]{:S(2)}) async-start(), calls=%async_computation.5 | async-start | bytes 2162688 | tf_op jit(solution)/shard_map/all_gather | solution.py:57
  106.5 6.5 %slice-start.8 = ((s8[7340032]{0:T(1024)(128)(4,1)}), s8[4194304]{0:T(1024)(128)(4,1)S(1)}, s32[]{:S(2)}) async-start(s8[7340032]{0:T(1024)(128)(4,1)} %bitcast.125), calls=%async_computation.18 | async-start | bytes 8388608
  115.9 150.2 %all-gather.13.cloned.1.call-start = ((), (), s32[]{:S(2)}) async-start(), calls=%async_computation.6 | async-start | bytes 2162688 | tf_op jit(solution)/shard_map/all_gather | solution.py:57
  171.7 40.6 %slice-start = ((s8[7340032]{0:T(1024)(128)(4,1)}), s8[3145728]{0:T(1024)(128)(4,1)S(1)}, s32[]{:S(2)}) async-start(s8[7340032]{0:T(1024)(128)(4,1)} %bitcast.117), calls=%async_computation.10 | async-start | bytes 6291456
  176.5 11.3 %copy-start = (bf16[128,256]{1,0:T(8,128)(2,1)S(1)}, bf16[128,256]{1,0:T(8,128)(2,1)}, u32[]{:S(2)}) copy-start(bf16[128,256]{1,0:T(8,128)(2,1)} %param.7) | copy-start | bytes 196612
  176.5 35.7 %slice-start.1 = ((s8[7340032]{0:T(1024)(128)(4,1)}), s8[4194304]{0:T(1024)(128)(4,1)S(1)}, s32[]{:S(2)}) async-start(s8[7340032]{0:T(1024)(128)(4,1)} %bitcast.117), calls=%async_computation.11 | async-start | bytes 8388608
  182.7 5.2 collective-permute-start
  188.0 26.5 %slice-start.10 = ((s8[7340032]{0:T(1024)(128)(4,1)}), s8[4194304]{0:T(1024)(128)(4,1)S(1)}, s32[]{:S(2)}) async-start(s8[7340032]{0:T(1024)(128)(4,1)} %bitcast.127), calls=%async_computation.20 | async-start | bytes 8388608
  217.4 146.9 %all-gather.15.cloned.1.call-start = ((), (), s32[]{:S(2)}) async-start(), calls=%async_computation.7 | async-start | bytes 2162688 | tf_op jit(solution)/shard_map/all_gather | solution.py:57
  270.2 40.3 %slice-start.2 = ((s8[7340032]{0:T(1024)(128)(4,1)}), s8[3145728]{0:T(1024)(128)(4,1)S(1)}, s32[]{:S(2)}) async-start(s8[7340032]{0:T(1024)(128)(4,1)} %bitcast.119), calls=%async_computation.12 | async-start | bytes 6291456
  275.0 35.5 %slice-start.3 = ((s8[7340032]{0:T(1024)(128)(4,1)}), s8[4194304]{0:T(1024)(128)(4,1)S(1)}, s32[]{:S(2)}) async-start(s8[7340032]{0:T(1024)(128)(4,1)} %bitcast.119), calls=%async_computation.13 | async-start | bytes 8388608
  281.1 5.2 collective-permute-start.1
  286.5 26.3 %slice-start.12 = ((s8[7340032]{0:T(1024)(128)(4,1)}), s8[4194304]{0:T(1024)(128)(4,1)S(1)}, s32[]{:S(2)}) async-start(s8[7340032]{0:T(1024)(128)(4,1)} %bitcast.129), calls=%async_computation.22 | async-start | bytes 8388608
  315.7 147.0 %all-gather.17.cloned.1.call-start = ((), (), s32[]{:S(2)}) async-start(), calls=%async_computation.8 | async-start | bytes 2162688 | tf_op jit(solution)/shard_map/all_gather | solution.py:57
  368.4 40.3 %slice-start.4 = ((s8[7340032]{0:T(1024)(128)(4,1)}), s8[3145728]{0:T(1024)(128)(4,1)S(1)}, s32[]{:S(2)}) async-start(s8[7340032]{0:T(1024)(128)(4,1)} %bitcast.121), calls=%async_computation.14 | async-start | bytes 6291456
  373.2 35.5 %slice-start.5 = ((s8[7340032]{0:T(1024)(128)(4,1)}), s8[4194304]{0:T(1024)(128)(4,1)S(1)}, s32[]{:S(2)}) async-start(s8[7340032]{0:T(1024)(128)(4,1)} %bitcast.121), calls=%async_computation.15 | async-start | bytes 8388608
  379.4 5.2 collective-permute-start.2
  384.7 26.3 %slice-start.14 = ((s8[7340032]{0:T(1024)(128)(4,1)}), s8[4194304]{0:T(1024)(128)(4,1)S(1)}, s32[]{:S(2)}) async-start(s8[7340032]{0:T(1024)(128)(4,1)} %bitcast.131), calls=%async_computation.24 | async-start | bytes 8388608
  413.9 147.0 %all-gather.19.cloned.1.call-start = ((), (), s32[]{:S(2)}) async-start(), calls=%async_computation.9 | async-start | bytes 2162688 | tf_op jit(solution)/shard_map/all_gather | solution.py:57
  466.7 40.4 %slice-start.6 = ((s8[7340032]{0:T(1024)(128)(4,1)}), s8[3145728]{0:T(1024)(128)(4,1)S(1)}, s32[]{:S(2)}) async-start(s8[7340032]{0:T(1024)(128)(4,1)} %bitcast.123), calls=%async_computation.16 | async-start | bytes 6291456
  471.5 35.6 %slice-start.7 = ((s8[7340032]{0:T(1024)(128)(4,1)}), s8[4194304]{0:T(1024)(128)(4,1)S(1)}, s32[]{:S(2)}) async-start(s8[7340032]{0:T(1024)(128)(4,1)} %bitcast.123), calls=%async_computation.17 | async-start | bytes 8388608
  477.7 5.2 collective-permute-start.3
  483.0 26.4 %slice-start.16 = ((s8[7340032]{0:T(1024)(128)(4,1)}), s8[4194304]{0:T(1024)(128)(4,1)S(1)}, s32[]{:S(2)}) async-start(s8[7340032]{0:T(1024)(128)(4,1)} %bitcast.133), calls=%async_computation.26 | async-start | bytes 8388608
  (6 other events, 17.9 us)
Sparse Core Ops, SparseCore 0:
  116.0 51.5 all-gather.10
  217.5 48.5 all-gather.12
  315.8 48.5 all-gather.14
  414.1 48.5 all-gather.16
  512.4 48.5 all-gather.18
